TPU v7x, 256 devices: a whole 4x4x8 slice. The times are simulated.
256 devices in a mesh: seq: 64 (over z, x, core), tp: 4 (over y).
Axes of the slice: x: 4, y: 4, z: 8, core: 2. Of those that a mesh axis runs over, the one named last changes fastest.
Arguments:
- hidden: bfloat16 [32768, 4096], P(('seq', 'tp')), may hold values from -640 to 640
- norm_gain: float32 [4096], replicated, may hold values from 0.5 to 1.5
- w_query: bfloat16 [4096, 2048], P(None, 'tp'), may hold values from -0.078125 to 0.078125
- w_key: bfloat16 [4096, 1024], P(None, 'tp'), may hold values from -2.421875 to 2.421875
- w_value: bfloat16 [4096, 1024], P(None, 'tp'), may hold values from -0.09375 to 0.09375
- doc_start: int32 [32768], P('seq'), may hold values from 0 to 32767, as said below
- block_owner: int32 [1024], P('seq'), may hold values from 0 to 63, as said below
Outputs:
- context_rows: bfloat16 [32768, 2048], P(('seq', 'tp'))
- key_cache: bfloat16 [49152, 1024], P('seq', 'tp')
- value_cache: bfloat16 [49152, 1024], P('seq', 'tp')
Inputs may be any that keep to these rules, and one draw needn't show every extreme that they name: `doc_start`: rows with equal values form one document: consecutive rows beginning at the row whose number is that value. Every document has at most 256 rows and one has exactly 256; all but the last have at least 64. `block_owner`: owner numbers never fall along the blocks. Owner o holds the blocks from o * 16 + e(o) up to (o + 1) * 16 + e(o + 1) - 1, where -4 <= e <= 4 and e is 0 at both ends of the axis; so an owner holds between 8 and 24 blocks, and some owner holds exactly 24.
All inputs are finite; a program needn't handle non-finite values.
Results may differ from a plain program's by a relative error of at most 0.0078.
Values may be sent and summed in bfloat16 or wider, within the bound.
No kernel may reach another device: no remote copies, remote signals or barrier semaphores. Data moves between devices by JAX's collectives and lax.ppermute only.
A program may use at most 128 MiB of HBM per device.

v0:
```python
import jax
import jax.numpy as jnp
from jax import lax
from jax.sharding import PartitionSpec as P

HD = 128
DOC_MAX = 256
EPS = 1e-05
ROPE_BASE = 500000.0


def from_behind(array, axis, by):
    length = lax.axis_size(axis)
    pairs = [(i, i + by) for i in range(length) if 0 <= i + by < length]
    return lax.ppermute(array, axis, pairs)


def rotate(packed, positions, head_count):
    row_count = packed.shape[0]
    head_width = packed.shape[1] // head_count
    half_width = head_width // 2
    frequency = jnp.power(
        ROPE_BASE, -jnp.arange(half_width, dtype=jnp.float32) * (2.0 / head_width)
    )
    angles = positions.astype(jnp.float32)[:, None] * frequency[None, :]
    cosine = jnp.cos(angles)[:, None, :]
    sine_part = jnp.sin(angles)[:, None, :]
    reshaped = packed.reshape(row_count, head_count, head_width)
    first_half = reshaped[:, :, :half_width]
    second = reshaped[:, :, half_width:]
    rotated = jnp.concatenate(
        [first_half * cosine - second * sine_part, second * cosine + first_half * sine_part], axis=2
    )
    return rotated.reshape(row_count, head_count * head_width)


def project(rows_in, norm_gain, w_query, w_key, w_value, positions):
    widened = rows_in.astype(jnp.float32)
    inverse_rms = lax.rsqrt(jnp.mean(widened * widened, axis=1, keepdims=True) + EPS)
    normed = (widened * inverse_rms * norm_gain[None, :]).astype(jnp.bfloat16)
    queries = jnp.dot(normed, w_query, preferred_element_type=jnp.float32)
    keys_f = jnp.dot(normed, w_key, preferred_element_type=jnp.float32)
    values_f = jnp.dot(normed, w_value, preferred_element_type=jnp.float32)
    queries = rotate(queries, positions, queries.shape[1] // HD).astype(jnp.bfloat16)
    keys_f = rotate(keys_f, positions, keys_f.shape[1] // HD).astype(jnp.bfloat16)
    return (queries, keys_f, values_f.astype(jnp.bfloat16))


def attend(
    queries, keys_in, values_in, query_doc, query_row, key_doc, key_row, key_live, offset, reach
):
    row_count = queries.shape[0]
    groups = keys_in.shape[1] // HD
    per_group = queries.shape[1] // keys_in.shape[1]
    window = row_count + reach

    def one_tile(index):
        first = index * row_count
        key_first = first + offset - reach
        near_keys = lax.dynamic_slice_in_dim(keys_in, key_first, window, 0)
        near_values = lax.dynamic_slice_in_dim(values_in, key_first, window, 0)
        near_doc = lax.dynamic_slice_in_dim(key_doc, key_first, window, 0)
        near_row = lax.dynamic_slice_in_dim(key_row, key_first, window, 0)
        near_live = lax.dynamic_slice_in_dim(key_live, key_first, window, 0)
        query_four = queries.reshape(row_count, groups, per_group, HD)
        key_three = near_keys.reshape(window, groups, HD)
        value_three = near_values.reshape(window, groups, HD)
        scores = jnp.einsum(
            "rgjd,kgd->gjrk", query_four, key_three, preferred_element_type=jnp.float32
        ) * HD ** (-0.5)
        allowed = (
            (query_doc[:, None] == near_doc[None, :])
            & (near_row[None, :] <= query_row[:, None])
            & (near_live[None, :] > 0)
        )
        allowed = allowed | (jnp.arange(window)[None, :] == jnp.arange(row_count)[:, None] + reach)
        scores = jnp.where(allowed[None, None], scores, -jnp.inf)
        highest = jnp.max(scores, axis=3, keepdims=True)
        weights = jnp.exp(scores - highest)
        weights = (weights / jnp.sum(weights, axis=3, keepdims=True)).astype(jnp.bfloat16)
        blended = jnp.einsum(
            "gjrk,kgd->rgjd", weights, value_three, preferred_element_type=jnp.float32
        )
        return blended.astype(jnp.bfloat16).reshape(row_count, groups * per_group * HD)

    tiles = lax.map(one_tile, jnp.arange(row_count // row_count, dtype=jnp.int32))
    return tiles.reshape(row_count, queries.shape[1])


def shards(hidden, norm_gain, w_query, w_key, w_value, doc_start, block_owner):
    home_hidden = lax.all_gather(hidden, "tp", axis=0, tiled=True)
    my_index = lax.axis_index("seq")
    home_rows = home_hidden.shape[0]
    home_blocks = block_owner.shape[0]
    block_rows = home_rows // home_blocks
    spill_rows = home_blocks // 4 * block_rows
    frame_size = home_rows + 2 * spill_rows
    all_rows = lax.axis_size("seq") * home_rows
    row_number = my_index * home_rows + jnp.arange(home_rows, dtype=jnp.int32)
    row_owner = jnp.repeat(block_owner, block_rows)
    frame_number = my_index * home_rows - spill_rows + jnp.arange(frame_size, dtype=jnp.int32)
    queries, keys_own, values_own = project(
        home_hidden, norm_gain, w_query, w_key, w_value, row_number - doc_start
    )
    left = from_behind((keys_own, values_own, doc_start), "seq", 1)
    left_live = jnp.ones((home_rows,), jnp.int32) * (my_index > 0).astype(jnp.int32)
    home_context = attend(
        queries,
        jnp.concatenate([left[0], keys_own], axis=0),
        jnp.concatenate([left[1], values_own], axis=0),
        doc_start,
        row_number,
        jnp.concatenate([left[2], doc_start], axis=0),
        jnp.concatenate([row_number - home_rows, row_number], axis=0),
        jnp.concatenate([left_live, jnp.ones((home_rows,), jnp.int32)], axis=0),
        home_rows,
        DOC_MAX,
    )
    arrived = []
    for direction in (1, -1):
        low_row = home_rows - spill_rows if direction == 1 else 0
        payload = (
            keys_own[low_row : low_row + spill_rows],
            values_own[low_row : low_row + spill_rows],
            row_owner[low_row : low_row + spill_rows],
        )
        arrived.append(from_behind((payload[0], payload[1], payload[2]), "seq", direction))
    from_left, from_right = arrived
    frame_keys = jnp.concatenate([from_left[0], keys_own, from_right[0]], axis=0)
    frame_values = jnp.concatenate([from_left[1], values_own, from_right[1]], axis=0)
    frame_owner = jnp.concatenate([from_left[2], row_owner, from_right[2]], axis=0)
    frame_live = (
        (frame_owner == my_index) & (frame_number >= 0) & (frame_number < all_rows)
    ).astype(jnp.int32)
    live_column = frame_live[:, None] > 0
    key_cache = jnp.where(live_column, frame_keys, jnp.zeros((), jnp.bfloat16))
    value_cache = jnp.where(live_column, frame_values, jnp.zeros((), jnp.bfloat16))
    context_rows = lax.all_to_all(home_context, "tp", split_axis=0, concat_axis=1, tiled=True)
    return (context_rows, key_cache, value_cache)


def solution(mesh):
    return jax.shard_map(
        shards,
        mesh=mesh,
        in_specs=(
            P(("seq", "tp"), None),
            P(),
            P(None, "tp"),
            P(None, "tp"),
            P(None, "tp"),
            P("seq"),
            P("seq"),
        ),
        out_specs=(P(("seq", "tp"), None), P("seq", "tp"), P("seq", "tp")),
        check_vma=False,
    )
```

profile of v0, /device:TPU:128, one launch (start us, length us, event | category | flops | bytes accessed | tf_op | source)
XLA Modules:
  0.0 141.9 jit_solution(14735143676403520581)
XLA Ops:
  7.2 0.0 copy-start
  7.2 0.0 copy-start.4
  7.2 0.0 all-gather.2.cloned.1.call-start
  7.2 0.7 all-gather.2.cloned.1.call-update
  7.9 0.8 fusion.35
  8.7 0.1 broadcast_in_dim.79
  8.8 0.1 slice.56
  8.9 3.6 %collective-permute-start.4 = (s32[128]{0:T(128)S(1)}, s32[128]{0:T(128)S(1)}, u32[]{:S(2)}, u32[]{:S(2)}) collective-permute-start(s32[128]{0:T(128)S(1)} %slice.56), channel_id=1, source_target_pairs={{4,0},{8,4},{12,8},{16,12},{20,16},{24,20},{28,24},{32,28},{36,32}... | collective-permute-start | bytes 1544 | tf_op jit(solution)/shard_map/ppermute | solution.py:15
  12.5 0.1 broadcast_in_dim.77
  12.6 0.1 slice.54
  12.7 1.9 %collective-permute-start.3 = (s32[128]{0:T(128)S(1)}, s32[128]{0:T(128)S(1)}, u32[]{:S(2)}, u32[]{:S(2)}) collective-permute-start(s32[128]{0:T(128)S(1)} %slice.54), channel_id=1, source_target_pairs={{0,4},{4,8},{8,12},{12,16},{16,20},{20,24},{24,28},{28,32},{32,36}... | collective-permute-start | bytes 1544 | tf_op jit(solution)/shard_map/ppermute | solution.py:15
  14.6 1.9 %collective-permute-start.1 = (s32[512]{0:T(512)}, s32[512]{0:T(512)S(1)}, u32[]{:S(2)}, u32[]{:S(2)}) collective-permute-start(s32[512]{0:T(512)} %param.12), channel_id=1, source_target_pairs={{0,4},{4,8},{8,12},{12,16},{16,20},{20,24},{24,28},{28,32},{32,36}... | collective-permute-start | bytes 6152 | tf_op jit(solution)/shard_map/ppermute | solution.py:15
  16.6 0.7 subtract_convert_fusion.2
  17.3 0.5 multiply_cosine_fusion
  17.9 0.7 broadcast_in_dim.78
  18.6 0.1 concatenate.45
  18.7 0.8 copy.30
  19.5 0.8 copy.32
  20.3 0.0 collective-permute-done.4
  20.3 0.6 collective-permute-done.3
  20.9 2.1 %collective-permute-done.1 = s32[512]{0:T(512)S(1)} collective-permute-done((s32[512]{0:T(512)}, s32[512]{0:T(512)S(1)}, u32[]{:S(2)}, u32[]{:S(2)}) %collective-permute-start.1) | collective-permute-done | bytes 2080 | tf_op jit(solution)/shard_map/ppermute | solution.py:15
  23.0 0.7 pad_add_fusion
  23.8 2.2 %fusion.9 = pred[512,768]{0,1:T(8,128)(4,1)} fusion(s32[512]{0:T(512)S(1)} %iota_add_fusion.1, s32[512]{0:T(512)S(1)} %get-tuple-element.62, s32[512]{0:T(512)} %param.12, s32[768]{0:T(1024)S(1)} %dynamic_slice.25, s32[768]{0:T(1024)S(1)} %dynamic_slice.24, pred[768]{0:T(1024)(128)(4,1)S(1)} %slice_compare_fusion), kind=kLoop, calls=%fused_computation.15 | loop fusion | flops 2359296 | bytes 406272 | tf_op jit(solution)/shard_map/while/body/eval_jaxpr/or | solution.py:76
  25.9 36.2 %all-gather.2.cloned.1.call-done = bf16[512,4096]{1,0:T(8,128)(2,1)} async-done(((bf16[128,4096]{1,0:T(8,128)(2,1)}), bf16[512,4096]{1,0:T(8,128)(2,1)}) %all-gather.2.cloned.1.call-update) | async-done | bytes 4194320 | tf_op jit(solution)/shard_map/all_gather | solution.py:91
  62.1 0.0 copy-start.1
  62.1 3.2 %fusion.1 = f32[512]{0:T(512)S(1)} fusion(bf16[512,4096]{1,0:T(8,128)(2,1)} %all-gather.2.cloned.1.call-done), kind=kLoop, calls=%fused_computation.3 | loop fusion | flops 6290944 | bytes 4196352 | tf_op jit(solution)/shard_map/reduce_sum | solution.py:39
  65.4 0.0 copy-done
  65.4 0.0 copy-done.4
  65.4 0.2 copy-done.1
  65.6 2.0 %convolution_convert_fusion = bf16[512,256]{1,0:T(8,128)(2,1)} fusion(bf16[4096,256]{1,0:T(8,128)(2,1)S(1)} %copy-done, bf16[512,4096]{1,0:T(8,128)(2,1)S(1)} %copy-done.1, f32[4096]{0:T(1024)S(1)} %copy-done.4, f32[512]{0:T(512)S(1)} %add_rsqrt_fusion), kind=kOutput, calls=%fused_computation.18 | convolution fusion | flops 1082261504 | bytes 6572032 | tf_op jit(solution)/shard_map/dot_general | solution.py:43
  67.6 0.9 fusion.34
  68.5 1.9 %collective-permute-start = (bf16[512,256]{1,0:T(8,128)(2,1)}, bf16[512,256]{1,0:T(8,128)(2,1)}, u32[]{:S(2)}, u32[]{:S(2)}) collective-permute-start(bf16[512,256]{1,0:T(8,128)(2,1)} %convolution_convert_fusion), channel_id=1, source_target_pairs={{0,4},{4,8},{8,12},{12,16},{16,20},{20,24},{24,28},{28,32},{32,36}... | collective-permute-start | bytes 786440 | tf_op jit(solution)/shard_map/ppermute | solution.py:15
  70.5 3.5 %collective-permute-start.7 = (bf16[128,256]{1,0:T(8,128)(2,1)S(1)}, bf16[128,256]{1,0:T(8,128)(2,1)}, u32[]{:S(2)}, u32[]{:S(2)}) collective-permute-start(bf16[128,256]{1,0:T(8,128)(2,1)S(1)} %get-tuple-element.49), channel_id=1, source_target_pairs={{0,4},{4,8},{8,12},{12,16},{16,20},{20,24},{24,28},{28,32},{32,36}... | collective-permute-start | bytes 196616 | tf_op jit(solution)/shard_map/ppermute | solution.py:15
  73.9 5.4 %collective-permute-start.8 = (bf16[128,256]{1,0:T(8,128)(2,1)S(1)}, bf16[128,256]{1,0:T(8,128)(2,1)}, u32[]{:S(2)}, u32[]{:S(2)}) collective-permute-start(bf16[128,256]{1,0:T(8,128)(2,1)S(1)} %get-tuple-element.50), channel_id=1, source_target_pairs={{4,0},{8,4},{12,8},{16,12},{20,16},{24,20},{28,24},{32,28},{36,32}... | collective-permute-start | bytes 196616 | tf_op jit(solution)/shard_map/ppermute | solution.py:15
  79.4 0.0 copy-done.3
  79.4 1.6 %fusion.30 = f32[512,256]{0,1:T(8,128)S(1)} fusion(bf16[4096,256]{1,0:T(8,128)(2,1)S(1)} %copy-done.3, bf16[512,4096]{1,0:T(8,128)(2,1)S(1)} %copy-done.1, f32[4096]{0:T(1024)S(1)} %copy-done.4, f32[512]{0:T(512)S(1)} %add_rsqrt_fusion), kind=kOutput, calls=%fused_computation.59 | convolution fusion | flops 1082130432 | bytes 6834176 | tf_op jit(solution)/shard_map/dot_general | solution.py:42
  81.0 0.8 fusion.33
  81.7 0.2 copy.46
  82.0 1.2 copy.45
  83.2 1.6 %subtract_convert_fusion.1 = (bf16[512,2,64]{2,1,0:T(2,128)(2,1)S(1)}, bf16[512,2,64]{2,1,0:T(2,128)(2,1)S(1)}) fusion(f32[512,2,64]{2,1,0:T(2,128)S(1)} %copy.46, f32[512,2,64]{2,1,0:T(2,128)S(1)} %copy.45, f32[512,64]{1,0:T(8,128)} %copy.32, f32[512,64]{1,0:T(8,128)} %copy.30), kind=kLoop, calls=%fused_computation.24 | loop fusion | flops 524288 | bytes 1048576 | tf_op jit(solution)/shard_map/convert.2
  84.7 0.7 pad_maximum_fusion.3
  85.5 1.9 %collective-permute-start.2 = (bf16[512,256]{1,0:T(8,128)(2,1)S(1)}, bf16[512,256]{1,0:T(8,128)(2,1)S(1)}, u32[]{:S(2)}, u32[]{:S(2)}) collective-permute-start(bf16[512,256]{1,0:T(8,128)(2,1)S(1)} %bitcast.51), channel_id=1, source_target_pairs={{0,4},{4,8},{8,12},{12,16},{16,20},{20,24},{24,28},{28,32},{32,36}... | collective-permute-start | bytes 786440 | tf_op jit(solution)/shard_map/ppermute | solution.py:15
  87.4 5.9 %fusion.28 = f32[512,512]{0,1:T(8,128)S(1)} fusion(bf16[4096,512]{1,0:T(8,128)(2,1)} %param.9, bf16[512,4096]{1,0:T(8,128)(2,1)} %all-gather.2.cloned.1.call-done, f32[4096]{0:T(1024)} %param.8, f32[512]{0:T(512)S(1)} %add_rsqrt_fusion), kind=kOutput, calls=%fused_computation.58 | convolution fusion | flops 2155872256 | bytes 9455616 | tf_op jit(solution)/shard_map/dot_general | solution.py:41
  93.4 0.2 subtract_convert_fusion
  93.6 0.4 slice_maximum_fusion.1
  94.0 7.0 %collective-permute-start.6 = (bf16[128,256]{1,0:T(8,128)(2,1)S(1)}, bf16[128,256]{1,0:T(8,128)(2,1)S(1)}, u32[]{:S(2)}, u32[]{:S(2)}) collective-permute-start(bf16[128,256]{1,0:T(8,128)(2,1)S(1)} %bitcast.60), channel_id=1, source_target_pairs={{4,0},{8,4},{12,8},{16,12},{20,16},{24,20},{28,24},{32,28},{36,32}... | collective-permute-start | bytes 196616 | tf_op jit(solution)/shard_map/ppermute | solution.py:15
  100.9 0.0 collective-permute-done.7
  100.9 2.1 %collective-permute-start.5 = (bf16[128,256]{1,0:T(8,128)(2,1)S(1)}, bf16[128,256]{1,0:T(8,128)(2,1)S(1)}, u32[]{:S(2)}, u32[]{:S(2)}) collective-permute-start(bf16[128,256]{1,0:T(8,128)(2,1)S(1)} %bitcast.59), channel_id=1, source_target_pairs={{0,4},{4,8},{8,12},{12,16},{16,20},{20,24},{24,28},{28,32},{32,36}... | collective-permute-start | bytes 196616 | tf_op jit(solution)/shard_map/ppermute | solution.py:15
  103.1 0.0 collective-permute-done.8
  103.1 0.0 collective-permute-done.6
  103.1 6.7 %collective-permute-done.5 = bf16[128,256]{1,0:T(8,128)(2,1)S(1)} collective-permute-done((bf16[128,256]{1,0:T(8,128)(2,1)S(1)}, bf16[128,256]{1,0:T(8,128)(2,1)S(1)}, u32[]{:S(2)}, u32[]{:S(2)}) %collective-permute-start.5) | collective-permute-done | bytes 65568 | tf_op jit(solution)/shard_map/ppermute | solution.py:15
  109.9 0.0 collective-permute-done
  109.9 0.0 collective-permute-done.2
  109.9 2.3 %maximum_select_fusion.1 = (bf16[768,256]{1,0:T(8,128)(2,1)}, bf16[768,256]{1,0:T(8,128)(2,1)S(1)}, bf16[768,256]{1,0:T(8,128)(2,1)S(1)}, bf16[768,256]{1,0:T(8,128)(2,1)}) fusion(bf16[128,256]{1,0:T(8,128)(2,1)} %collective-permute-done.8, bf16[512,256]{1,0:T(8,128)(2,1)} %convolution_convert_fusion, bf16[128,256]{1,0:T(8,128)(2,1)} %collective-permute-done.7, ...), kind=kLoop, calls=%fused_computation.28 | loop fusion | flops 4325376 | bytes 2884352 | tf_op jit(solution)/shard_map/jit(_where)/select_n | solution.py:137
  112.1 0.9 copy.42
  113.1 0.1 reshape.241
  113.2 0.0 copy-start.2
  113.2 6.1 %fusion.36 = (f32[2,2,512]{2,1,0:T(2,128)S(1)}, f32[2,2,512,768]{2,3,1,0:T(8,128)}) fusion(pred[512,768]{0,1:T(8,128)(4,1)} %fusion.9, bf16[512,2,2,128]{0,3,2,1:T(8,128)(2,1)S(1)} %bitcast.53, bf16[768,2,128,1]{2,1,0,3:T(2,128)(2,1)S(1)} %bitcast.56), kind=kOutput, calls=%fused_computation.63 | convolution fusion | flops 408945408 | bytes 7610368 | tf_op jit(solution)/shard_map/while/body/eval_jaxpr/sub | solution.py:79
  119.3 0.0 copy-done.2
  119.3 3.4 %fusion.11 = bf16[512,2,2,128]{0,3,2,1:T(8,128)(2,1)S(1)} fusion(bf16[768,2,128,1]{0,2,3,1:T(8,128)(2,1)S(1)} %bitcast.55, f32[2,2,512,768]{2,3,1,0:T(8,128)} %get-tuple-element.60, f32[2,2,512]{2,1,0:T(2,128)S(1)} %get-tuple-element.59), kind=kOutput, calls=%fused_computation.17 | convolution fusion | flops 406061056 | bytes 7217152 | tf_op jit(solution)/shard_map/while/body/eval_jaxpr/gjrk,kgd->rgjd/dot_general | solution.py:81
  122.6 0.1 all_to_all.14
  122.8 0.1 copy.37
  122.9 11.2 %all_to_all.19 = bf16[4,128,512]{1,2,0:T(8,128)(2,1)S(1)} all-to-all(bf16[4,128,512]{1,2,0:T(8,128)(2,1)S(1)} %copy.37), channel_id=1, replica_groups=mesh['seq'=64,'tp'=4] {'tp'}, dimensions={0} | all-to-all | bytes 1048576 | tf_op jit(solution)/shard_map/all_to_all | solution.py:138
  134.1 1.0 copy.38
  (15 shorter events, 0.2 us)
Async XLA Ops:
  7.2 58.2 %copy-start = (bf16[4096,256]{1,0:T(8,128)(2,1)S(1)}, bf16[4096,256]{1,0:T(8,128)(2,1)}, u32[]{:S(2)}) copy-start(bf16[4096,256]{1,0:T(8,128)(2,1)} %param.11) | copy-start | bytes 6291460
  7.2 58.2 %copy-start.4 = (f32[4096]{0:T(1024)S(1)}, f32[4096]{0:T(1024)}, u32[]{:S(2)}) copy-start(f32[4096]{0:T(1024)} %param.8) | copy-start | bytes 49156
  7.2 54.9 %all-gather.2.cloned.1.call-start = ((), (), s32[]{:S(2)}) async-start(), calls=%async_computation.1 | async-start | bytes 5242880 | tf_op jit(solution)/shard_map/all_gather | solution.py:91
  8.9 11.4 %collective-permute-start.4 = (s32[128]{0:T(128)S(1)}, s32[128]{0:T(128)S(1)}, u32[]{:S(2)}, u32[]{:S(2)}) collective-permute-start(s32[128]{0:T(128)S(1)} %slice.56), channel_id=1, source_target_pairs={{4,0},{8,4},{12,8},{16,12},{20,16},{24,20},{28,24},{32,28},{36,32}... | collective-permute-start | bytes 1544 | tf_op jit(solution)/shard_map/ppermute | solution.py:15
  12.7 8.2 %collective-permute-start.3 = (s32[128]{0:T(128)S(1)}, s32[128]{0:T(128)S(1)}, u32[]{:S(2)}, u32[]{:S(2)}) collective-permute-start(s32[128]{0:T(128)S(1)} %slice.54), channel_id=1, source_target_pairs={{0,4},{4,8},{8,12},{12,16},{16,20},{20,24},{24,28},{28,32},{32,36}... | collective-permute-start | bytes 1544 | tf_op jit(solution)/shard_map/ppermute | solution.py:15
  14.6 8.4 %collective-permute-start.1 = (s32[512]{0:T(512)}, s32[512]{0:T(512)S(1)}, u32[]{:S(2)}, u32[]{:S(2)}) collective-permute-start(s32[512]{0:T(512)} %param.12), channel_id=1, source_target_pairs={{0,4},{4,8},{8,12},{12,16},{16,20},{20,24},{24,28},{28,32},{32,36}... | collective-permute-start | bytes 6152 | tf_op jit(solution)/shard_map/ppermute | solution.py:15
  62.1 3.4 %copy-start.1 = (bf16[512,4096]{1,0:T(8,128)(2,1)S(1)}, bf16[512,4096]{1,0:T(8,128)(2,1)}, u32[]{:S(2)}) copy-start(bf16[512,4096]{1,0:T(8,128)(2,1)} %all-gather.2.cloned.1.call-done) | copy-start | bytes 12582916
  65.6 13.8 %copy-start.3 = (bf16[4096,256]{1,0:T(8,128)(2,1)S(1)}, bf16[4096,256]{1,0:T(8,128)(2,1)}, u32[]{:S(2)}) copy-start(bf16[4096,256]{1,0:T(8,128)(2,1)} %param.10) | copy-start | bytes 6291460
  68.5 41.3 %collective-permute-start = (bf16[512,256]{1,0:T(8,128)(2,1)}, bf16[512,256]{1,0:T(8,128)(2,1)}, u32[]{:S(2)}, u32[]{:S(2)}) collective-permute-start(bf16[512,256]{1,0:T(8,128)(2,1)} %convolution_convert_fusion), channel_id=1, source_target_pairs={{0,4},{4,8},{8,12},{12,16},{16,20},{20,24},{24,28},{28,32},{32,36}... | collective-permute-start | bytes 786440 | tf_op jit(solution)/shard_map/ppermute | solution.py:15
  70.5 30.5 %collective-permute-start.7 = (bf16[128,256]{1,0:T(8,128)(2,1)S(1)}, bf16[128,256]{1,0:T(8,128)(2,1)}, u32[]{:S(2)}, u32[]{:S(2)}) collective-permute-start(bf16[128,256]{1,0:T(8,128)(2,1)S(1)} %get-tuple-element.49), channel_id=1, source_target_pairs={{0,4},{4,8},{8,12},{12,16},{16,20},{20,24},{24,28},{28,32},{32,36}... | collective-permute-start | bytes 196616 | tf_op jit(solution)/shard_map/ppermute | solution.py:15
  73.9 29.2 %collective-permute-start.8 = (bf16[128,256]{1,0:T(8,128)(2,1)S(1)}, bf16[128,256]{1,0:T(8,128)(2,1)}, u32[]{:S(2)}, u32[]{:S(2)}) collective-permute-start(bf16[128,256]{1,0:T(8,128)(2,1)S(1)} %get-tuple-element.50), channel_id=1, source_target_pairs={{4,0},{8,4},{12,8},{16,12},{20,16},{24,20},{28,24},{32,28},{36,32}... | collective-permute-start | bytes 196616 | tf_op jit(solution)/shard_map/ppermute | solution.py:15
  85.5 24.4 %collective-permute-start.2 = (bf16[512,256]{1,0:T(8,128)(2,1)S(1)}, bf16[512,256]{1,0:T(8,128)(2,1)S(1)}, u32[]{:S(2)}, u32[]{:S(2)}) collective-permute-start(bf16[512,256]{1,0:T(8,128)(2,1)S(1)} %bitcast.51), channel_id=1, source_target_pairs={{0,4},{4,8},{8,12},{12,16},{16,20},{20,24},{24,28},{28,32},{32,36}... | collective-permute-start | bytes 786440 | tf_op jit(solution)/shard_map/ppermute | solution.py:15
  94.0 9.1 %collective-permute-start.6 = (bf16[128,256]{1,0:T(8,128)(2,1)S(1)}, bf16[128,256]{1,0:T(8,128)(2,1)S(1)}, u32[]{:S(2)}, u32[]{:S(2)}) collective-permute-start(bf16[128,256]{1,0:T(8,128)(2,1)S(1)} %bitcast.60), channel_id=1, source_target_pairs={{4,0},{8,4},{12,8},{16,12},{20,16},{24,20},{28,24},{32,28},{36,32}... | collective-permute-start | bytes 196616 | tf_op jit(solution)/shard_map/ppermute | solution.py:15
  100.9 8.9 %collective-permute-start.5 = (bf16[128,256]{1,0:T(8,128)(2,1)S(1)}, bf16[128,256]{1,0:T(8,128)(2,1)S(1)}, u32[]{:S(2)}, u32[]{:S(2)}) collective-permute-start(bf16[128,256]{1,0:T(8,128)(2,1)S(1)} %bitcast.59), channel_id=1, source_target_pairs={{0,4},{4,8},{8,12},{12,16},{16,20},{20,24},{24,28},{28,32},{32,36}... | collective-permute-start | bytes 196616 | tf_op jit(solution)/shard_map/ppermute | solution.py:15
  113.2 6.1 %copy-start.2 = (bf16[768,256]{0,1:T(8,128)(2,1)S(1)}, bf16[768,256]{0,1:T(8,128)(2,1)}, u32[]{:S(2)}) copy-start(bf16[768,256]{0,1:T(8,128)(2,1)} %copy.42) | copy-start | bytes 1179652
Sparse Core Ops, SparseCore 0:
  9.8 52.2 all-gather.1
where the time goes:
time: 143 us; the launch traced here: 142 us
  waiting for transfers between devices  46.3 us (32%)
  starting transfers between devices  29.3 us (20%)
  matrix products  19.1 us (13%)
  between operations  14.4 us (10%)
  other arithmetic  12.5 us (9%)
  blocking collectives  11.2 us (8%)
  local copies, waits for them, and re-layouts  9.14 us (6%)
    all_gather x1, waiting for transfers between devices, shards(): home_hidden = lax.all_gather(hidden, 'tp', axis=0, tiled=True)  36.2 us
    ppermute x9, starting transfers between devices, from_behind(): return lax.ppermute(array, axis, pairs)  29.3 us
    all_to_all x1, blocking collectives, shards(): lax.all_to_all(home_context, 'tp', split_axis=0, concat_axis=1, tiled=True)  11.2 us
    ppermute x9, waiting for transfers between devices, from_behind(): return lax.ppermute(array, axis, pairs)  9.44 us
    sub x1, matrix products, one_tile(): weights = jnp.exp(scores - highest)  6.09 us
    dot_general x1, matrix products, project(): queries = jnp.dot(normed, w_query, preferred_element_type=jnp.float32)  5.94 us
    dot_general x1, matrix products, one_tile(): jnp.einsum('gjrk,kgd->rgjd', weights, value_three, preferred_element_type...  3.37 us
    reduce_sum x1, other arithmetic, project(): jnp.mean(widened * widened, axis=1, keepdims=True) + EPS  3.23 us
  transfers between devices with their start and end apart: 10, of which 4 were waited for; matrix products, arithmetic and copies ran while one was open for 14% of the time, Pallas kernels for 0%

commit v1 on v0

--- a/solution.py
+++ b/solution.py
@@ -135,7 +135,22 @@
     live_column = frame_live[:, None] > 0
     key_cache = jnp.where(live_column, frame_keys, jnp.zeros((), jnp.bfloat16))
     value_cache = jnp.where(live_column, frame_values, jnp.zeros((), jnp.bfloat16))
-    context_rows = lax.all_to_all(home_context, "tp", split_axis=0, concat_axis=1, tiled=True)
+    seen_now = lax.psum(1, axis_name="tp")
+    aux = lax.axis_index("tp")
+    front, d_next = (seen_now, aux)
+    prior = home_context.shape[0] // front
+    extra = list(home_context.shape)
+    extra[0] = prior
+    r_now = extra[1]
+    extra[1] = r_now * front
+    context_rows = jnp.zeros(extra, home_context.dtype)
+    for ix in range(front):
+        block_next = lax.dynamic_slice_in_dim(home_context, (d_next ^ ix) * prior, prior, axis=0)
+        if ix:
+            block_next = lax.ppermute(block_next, "tp", perm=[(jj, jj ^ ix) for jj in range(front)])
+        context_rows = lax.dynamic_update_slice_in_dim(
+            context_rows, block_next, (d_next ^ ix) * r_now, axis=1
+        )
     return (context_rows, key_cache, value_cache)
 
 

time: 143 us -> 134 us (0.937)
  blocking collectives: 11.2 us -> 0 us
  starting transfers between devices: 29.3 us -> 37.6 us
  waiting for transfers between devices: 46.3 us -> 41.8 us
    all_to_all x1 -> x0, blocking collectives: 11.2 us -> none  [shards(): lax.all_to_all(home_context, 'tp', split_axis=0, concat_axis=1, tiled=True)]
    ppermute x9, waiting for transfers between devices: 9.44 us -> 4.32 us  [from_behind(): return lax.ppermute(array, axis, pairs)]
    ppermute x0 -> x3, starting transfers between devices: none -> 4.96 us  [shards(): lax.ppermute(block_next, 'tp', perm=[(jj, jj ^ ix) for jj in range(front)])]
    ppermute x0 -> x3, waiting for transfers between devices: none -> 3.9 us  [shards(): lax.ppermute(block_next, 'tp', perm=[(jj, jj ^ ix) for jj in range(front)])]
    dot_general x1, matrix products: 5.94 us -> 2.6 us  [project(): queries = jnp.dot(normed, w_query, preferred_element_type=jnp.float32)]
    ppermute x9, starting transfers between devices: 29.3 us -> 32.6 us  [from_behind(): return lax.ppermute(array, axis, pairs)]
    all_gather x1, waiting for transfers between devices: 36.2 us -> 32.9 us  [shards(): home_hidden = lax.all_gather(hidden, 'tp', axis=0, tiled=True)]
    dot_general x1, matrix products: 2.05 us -> 4.31 us  [project(): values_f = jnp.dot(normed, w_value, preferred_element_type=jnp.float32)]
  transfers between devices with their start and end apart: 10 -> 13, of which waited for: 4 -> 5; matrix products, arithmetic and copies ran while one was open for 14% -> 8% of each run, Pallas kernels for 0% -> 0%
where the time goes in v1:
time: 134 us; the launch traced here: 132 us
  waiting for transfers between devices  41.8 us (31%)
  starting transfers between devices  37.6 us (28%)
  matrix products  18 us (13%)
  between operations  14.5 us (11%)
  other arithmetic  11.3 us (8%)
  local copies, waits for them, and re-layouts  8.54 us (6%)
    all_gather x1, waiting for transfers between devices, shards(): home_hidden = lax.all_gather(hidden, 'tp', axis=0, tiled=True)  32.9 us
    ppermute x9, starting transfers between devices, from_behind(): return lax.ppermute(array, axis, pairs)  32.6 us
    sub x1, matrix products, one_tile(): weights = jnp.exp(scores - highest)  6.16 us
    ppermute x3, starting transfers between devices, shards(): lax.ppermute(block_next, 'tp', perm=[(jj, jj ^ ix) for jj in range(front)])  4.96 us
    ppermute x9, waiting for transfers between devices, from_behind(): return lax.ppermute(array, axis, pairs)  4.32 us
    dot_general x1, matrix products, project(): values_f = jnp.dot(normed, w_value, preferred_element_type=jnp.float32)  4.31 us
    ppermute x3, waiting for transfers between devices, shards(): lax.ppermute(block_next, 'tp', perm=[(jj, jj ^ ix) for jj in range(front)])  3.9 us
    dot_general x1, matrix products, one_tile(): jnp.einsum('gjrk,kgd->rgjd', weights, value_three, preferred_element_type...  3.37 us
  transfers between devices with their start and end apart: 13, of which 5 were waited for; matrix products, arithmetic and copies ran while one was open for 8% of the time, Pallas kernels for 0%

profile of v1, /device:TPU:128, one launch (start us, length us, event | category | flops | bytes accessed | tf_op | source)
XLA Modules:
  0.0 131.8 jit_solution(3380435688488272077)
XLA Ops:
  7.2 0.0 copy-start
  7.2 0.0 all-gather.2.cloned.1.call-start
  7.2 0.7 all-gather.2.cloned.1.call-update
  7.9 0.8 fusion.34
  8.7 0.1 broadcast_in_dim.81
  8.8 0.1 slice.54
  8.9 1.9 %collective-permute-start.6 = (s32[128]{0:T(128)S(1)}, s32[128]{0:T(128)S(1)}, u32[]{:S(2)}, u32[]{:S(2)}) collective-permute-start(s32[128]{0:T(128)S(1)} %slice.54), channel_id=1, source_target_pairs={{0,4},{4,8},{8,12},{12,16},{16,20},{20,24},{24,28},{28,32},{32,36}... | collective-permute-start | bytes 1544 | tf_op jit(solution)/shard_map/ppermute | solution.py:15
  10.8 0.1 broadcast_in_dim.83
  10.9 0.1 slice.56
  11.0 7.0 %collective-permute-start.7 = (s32[128]{0:T(128)S(1)}, s32[128]{0:T(128)S(1)}, u32[]{:S(2)}, u32[]{:S(2)}) collective-permute-start(s32[128]{0:T(128)S(1)} %slice.56), channel_id=1, source_target_pairs={{4,0},{8,4},{12,8},{16,12},{20,16},{24,20},{28,24},{32,28},{36,32}... | collective-permute-start | bytes 1544 | tf_op jit(solution)/shard_map/ppermute | solution.py:15
  17.9 1.9 %collective-permute-start.1 = (s32[512]{0:T(512)}, s32[512]{0:T(512)S(1)}, u32[]{:S(2)}, u32[]{:S(2)}) collective-permute-start(s32[512]{0:T(512)} %param.12), channel_id=1, source_target_pairs={{0,4},{4,8},{8,12},{12,16},{16,20},{20,24},{24,28},{28,32},{32,36}... | collective-permute-start | bytes 6152 | tf_op jit(solution)/shard_map/ppermute | solution.py:15
  19.9 0.7 subtract_convert_fusion.2
  20.6 0.5 multiply_cosine_fusion
  21.1 0.8 copy.23
  22.0 0.8 copy.25
  22.8 0.7 broadcast_in_dim.82
  23.6 0.1 concatenate.45
  23.7 0.0 collective-permute-done.6
  23.7 0.0 collective-permute-done.7
  23.7 2.7 %collective-permute-done.1 = s32[512]{0:T(512)S(1)} collective-permute-done((s32[512]{0:T(512)}, s32[512]{0:T(512)S(1)}, u32[]{:S(2)}, u32[]{:S(2)}) %collective-permute-start.1) | collective-permute-done | bytes 2080 | tf_op jit(solution)/shard_map/ppermute | solution.py:15
  26.4 0.7 pad_add_fusion
  27.1 2.2 %fusion.9 = pred[512,768]{0,1:T(8,128)(4,1)} fusion(s32[512]{0:T(512)S(1)} %iota_add_fusion.1, s32[512]{0:T(512)S(1)} %get-tuple-element.60, s32[512]{0:T(512)} %param.12, s32[768]{0:T(1024)S(1)} %dynamic_slice.37, s32[768]{0:T(1024)S(1)} %dynamic_slice.36, pred[768]{0:T(1024)(128)(4,1)S(1)} %slice_compare_fusion), kind=kLoop, calls=%fused_computation.15 | loop fusion | flops 2359296 | bytes 406272 | tf_op jit(solution)/shard_map/while/body/eval_jaxpr/or | solution.py:76
  29.2 32.9 %all-gather.2.cloned.1.call-done = bf16[512,4096]{1,0:T(8,128)(2,1)} async-done(((bf16[128,4096]{1,0:T(8,128)(2,1)}), bf16[512,4096]{1,0:T(8,128)(2,1)}) %all-gather.2.cloned.1.call-update) | async-done | bytes 4194320 | tf_op jit(solution)/shard_map/all_gather | solution.py:91
  62.1 3.2 %fusion.1 = f32[512]{0:T(512)S(1)} fusion(bf16[512,4096]{1,0:T(8,128)(2,1)} %all-gather.2.cloned.1.call-done), kind=kLoop, calls=%fused_computation.3 | loop fusion | flops 6290944 | bytes 4196352 | tf_op jit(solution)/shard_map/reduce_sum | solution.py:39
  65.4 0.2 copy-done.1
  65.6 1.6 %fusion.29 = f32[512,256]{0,1:T(8,128)S(1)} fusion(bf16[4096,256]{1,0:T(8,128)(2,1)S(1)} %copy-done, bf16[512,4096]{1,0:T(8,128)(2,1)S(1)} %copy-done.1, f32[4096]{0:T(1024)S(1)} %copy-done.5, f32[512]{0:T(512)S(1)} %add_rsqrt_fusion), kind=kOutput, calls=%fused_computation.66 | convolution fusion | flops 1082130432 | bytes 6834176 | tf_op jit(solution)/shard_map/dot_general | solution.py:42
  67.2 0.8 fusion.32
  67.9 0.2 copy.40
  68.2 1.2 copy.41
  69.4 1.6 %subtract_convert_fusion.1 = (bf16[512,2,64]{2,1,0:T(2,128)(2,1)S(1)}, bf16[512,2,64]{2,1,0:T(2,128)(2,1)S(1)}) fusion(f32[512,2,64]{2,1,0:T(2,128)S(1)} %copy.41, f32[512,2,64]{2,1,0:T(2,128)S(1)} %copy.40, f32[512,64]{1,0:T(8,128)} %copy.25, f32[512,64]{1,0:T(8,128)} %copy.23), kind=kLoop, calls=%fused_computation.23 | loop fusion | flops 524288 | bytes 1048576 | tf_op jit(solution)/shard_map/convert.2
  71.0 0.4 slice_maximum_fusion.1
  71.3 0.7 pad_maximum_fusion.3
  72.0 0.0 copy-start.4
  72.1 4.3 %convolution_convert_fusion = bf16[512,256]{1,0:T(8,128)(2,1)S(1)} fusion(bf16[4096,256]{1,0:T(8,128)(2,1)} %param.11, bf16[512,4096]{1,0:T(8,128)(2,1)} %all-gather.2.cloned.1.call-done, f32[4096]{0:T(1024)S(1)} %copy-done.5, f32[512]{0:T(512)S(1)} %add_rsqrt_fusion), kind=kOutput, calls=%fused_computation.17 | convolution fusion | flops 1082261504 | bytes 6572032 | tf_op jit(solution)/shard_map/dot_general | solution.py:43
  76.4 1.9 %collective-permute-start = (bf16[512,256]{1,0:T(8,128)(2,1)S(1)}, bf16[512,256]{1,0:T(8,128)(2,1)S(1)}, u32[]{:S(2)}, u32[]{:S(2)}) collective-permute-start(bf16[512,256]{1,0:T(8,128)(2,1)S(1)} %convolution_convert_fusion), channel_id=1, source_target_pairs={{0,4},{4,8},{8,12},{12,16},{16,20},{20,24},{24,28},{28,32},{32,36}... | collective-permute-start | bytes 786440 | tf_op jit(solution)/shard_map/ppermute | solution.py:15
  78.3 3.5 %collective-permute-start.8 = (bf16[128,256]{1,0:T(8,128)(2,1)S(1)}, bf16[128,256]{1,0:T(8,128)(2,1)S(1)}, u32[]{:S(2)}, u32[]{:S(2)}) collective-permute-start(bf16[128,256]{1,0:T(8,128)(2,1)S(1)} %bitcast.54), channel_id=1, source_target_pairs={{0,4},{4,8},{8,12},{12,16},{16,20},{20,24},{24,28},{28,32},{32,36}... | collective-permute-start | bytes 196616 | tf_op jit(solution)/shard_map/ppermute | solution.py:15
  81.8 5.4 %collective-permute-start.9 = (bf16[128,256]{1,0:T(8,128)(2,1)S(1)}, bf16[128,256]{1,0:T(8,128)(2,1)S(1)}, u32[]{:S(2)}, u32[]{:S(2)}) collective-permute-start(bf16[128,256]{1,0:T(8,128)(2,1)S(1)} %bitcast.53), channel_id=1, source_target_pairs={{4,0},{8,4},{12,8},{16,12},{20,16},{24,20},{28,24},{32,28},{36,32}... | collective-permute-start | bytes 196616 | tf_op jit(solution)/shard_map/ppermute | solution.py:15
  87.3 1.9 %collective-permute-start.2 = (bf16[512,256]{1,0:T(8,128)(2,1)S(1)}, bf16[512,256]{1,0:T(8,128)(2,1)S(1)}, u32[]{:S(2)}, u32[]{:S(2)}) collective-permute-start(bf16[512,256]{1,0:T(8,128)(2,1)S(1)} %bitcast.44), channel_id=1, source_target_pairs={{0,4},{4,8},{8,12},{12,16},{16,20},{20,24},{24,28},{28,32},{32,36}... | collective-permute-start | bytes 786440 | tf_op jit(solution)/shard_map/ppermute | solution.py:15
  89.2 1.9 %collective-permute-start.10 = (bf16[128,256]{1,0:T(8,128)(2,1)S(1)}, bf16[128,256]{1,0:T(8,128)(2,1)S(1)}, u32[]{:S(2)}, u32[]{:S(2)}) collective-permute-start(bf16[128,256]{1,0:T(8,128)(2,1)S(1)} %get-tuple-element.47), channel_id=1, source_target_pairs={{0,4},{4,8},{8,12},{12,16},{16,20},{20,24},{24,28},{28,32},{32,36}... | collective-permute-start | bytes 196616 | tf_op jit(solution)/shard_map/ppermute | solution.py:15
  91.2 2.6 %fusion.27 = f32[512,512]{0,1:T(8,128)S(1)} fusion(bf16[4096,512]{1,0:T(8,128)(2,1)S(1)} %copy-done.4, bf16[512,4096]{1,0:T(8,128)(2,1)S(1)} %copy-done.2, f32[4096]{0:T(1024)S(1)} %copy-done.5, f32[512]{0:T(512)S(1)} %add_rsqrt_fusion), kind=kOutput, calls=%fused_computation.65 | convolution fusion | flops 2155872256 | bytes 9455616 | tf_op jit(solution)/shard_map/dot_general | solution.py:41
  93.8 0.2 subtract_convert_fusion
  94.0 0.0 collective-permute-done.8
  94.0 7.1 %collective-permute-start.11 = (bf16[128,256]{1,0:T(8,128)(2,1)S(1)}, bf16[128,256]{1,0:T(8,128)(2,1)S(1)}, u32[]{:S(2)}, u32[]{:S(2)}) collective-permute-start(bf16[128,256]{1,0:T(8,128)(2,1)S(1)} %get-tuple-element.48), channel_id=1, source_target_pairs={{4,0},{8,4},{12,8},{16,12},{20,16},{24,20},{28,24},{32,28},{36,32}... | collective-permute-start | bytes 196616 | tf_op jit(solution)/shard_map/ppermute | solution.py:15
  101.2 0.0 collective-permute-done.9
  101.2 0.0 collective-permute-done.10
  101.2 1.6 %collective-permute-done.11 = bf16[128,256]{1,0:T(8,128)(2,1)S(1)} collective-permute-done((bf16[128,256]{1,0:T(8,128)(2,1)S(1)}, bf16[128,256]{1,0:T(8,128)(2,1)S(1)}, u32[]{:S(2)}, u32[]{:S(2)}) %collective-permute-start.11) | collective-permute-done | bytes 65568 | tf_op jit(solution)/shard_map/ppermute | solution.py:15
  102.9 1.1 maximum_select_fusion.1
  104.0 0.8 reshape.239
  104.8 0.2 copy.37
  105.0 6.2 %fusion.35 = (f32[2,2,512]{2,1,0:T(2,128)S(1)}, f32[2,2,512,768]{2,3,1,0:T(8,128)}) fusion(pred[512,768]{0,1:T(8,128)(4,1)} %fusion.9, bf16[512,2,2,128]{0,3,2,1:T(8,128)(2,1)S(1)} %bitcast.46, bf16[768,2,128,1]{2,1,0,3:T(2,128)(2,1)} %bitcast.50), kind=kOutput, calls=%fused_computation.70 | convolution fusion | flops 408945408 | bytes 7610368 | tf_op jit(solution)/shard_map/while/body/eval_jaxpr/sub | solution.py:79
  111.2 3.4 %fusion.10 = bf16[2,128,2,512]{3,1,2,0:T(8,128)(2,1)S(1)} fusion(bf16[768,2,128,1]{0,2,3,1:T(8,128)(2,1)S(1)} %bitcast.49, f32[2,2,512,768]{2,3,1,0:T(8,128)} %get-tuple-element.58, f32[2,2,512]{2,1,0:T(2,128)S(1)} %get-tuple-element.57), kind=kOutput, calls=%fused_computation.16 | convolution fusion | flops 406061056 | bytes 7217152 | tf_op jit(solution)/shard_map/while/body/eval_jaxpr/gjrk,kgd->rgjd/dot_general | solution.py:81
  114.5 0.1 constant_dynamic-slice_fusion
  114.7 0.1 copy.43
  114.8 0.9 collective-permute-start.3
  115.7 0.1 copy.42
  115.8 0.1 copy.44
  115.9 1.8 %collective-permute-start.4 = (bf16[128,512]{1,0:T(8,128)(2,1)S(1)}, bf16[128,512]{1,0:T(8,128)(2,1)S(1)}, u32[]{:S(2)}, u32[]{:S(2)}) collective-permute-start(bf16[128,512]{1,0:T(8,128)(2,1)S(1)} %copy.44), channel_id=1, source_target_pairs={{0,2},{1,3},{2,0},{3,1},{4,6},{5,7},{6,4},{7,5},{8,10},{9,11},{10,... | collective-permute-start | bytes 393224 | tf_op jit(solution)/shard_map/ppermute | solution.py:150
  117.7 0.1 copy.45
  117.9 2.2 %collective-permute-start.5 = (bf16[128,512]{1,0:T(8,128)(2,1)S(1)}, bf16[128,512]{1,0:T(8,128)(2,1)S(1)}, u32[]{:S(2)}, u32[]{:S(2)}) collective-permute-start(bf16[128,512]{1,0:T(8,128)(2,1)S(1)} %copy.45), channel_id=1, source_target_pairs={{0,3},{1,2},{2,1},{3,0},{4,7},{5,6},{6,5},{7,4},{8,11},{9,10},{10,... | collective-permute-start | bytes 393224 | tf_op jit(solution)/shard_map/ppermute | solution.py:150
  120.2 0.0 collective-permute-done.3
  120.2 2.3 %collective-permute-done.4 = bf16[128,512]{1,0:T(8,128)(2,1)S(1)} collective-permute-done((bf16[128,512]{1,0:T(8,128)(2,1)S(1)}, bf16[128,512]{1,0:T(8,128)(2,1)S(1)}, u32[]{:S(2)}, u32[]{:S(2)}) %collective-permute-start.4) | collective-permute-done | bytes 131104 | tf_op jit(solution)/shard_map/ppermute | solution.py:150
  122.5 1.6 %collective-permute-done.5 = bf16[128,512]{1,0:T(8,128)(2,1)S(1)} collective-permute-done((bf16[128,512]{1,0:T(8,128)(2,1)S(1)}, bf16[128,512]{1,0:T(8,128)(2,1)S(1)}, u32[]{:S(2)}, u32[]{:S(2)}) %collective-permute-start.5) | collective-permute-done | bytes 131104 | tf_op jit(solution)/shard_map/ppermute | solution.py:150
  124.1 0.0 copy-start.3
  124.2 0.8 copy-done.3
  (29 shorter events, 0.3 us)
Async XLA Ops:
  7.2 58.2 %copy-start = (bf16[4096,256]{1,0:T(8,128)(2,1)S(1)}, bf16[4096,256]{1,0:T(8,128)(2,1)}, u32[]{:S(2)}) copy-start(bf16[4096,256]{1,0:T(8,128)(2,1)} %param.10) | copy-start | bytes 6291460
  7.2 58.2 %copy-start.5 = (f32[4096]{0:T(1024)S(1)}, f32[4096]{0:T(1024)}, u32[]{:S(2)}) copy-start(f32[4096]{0:T(1024)} %param.8) | copy-start | bytes 49156
  7.2 54.9 %all-gather.2.cloned.1.call-start = ((), (), s32[]{:S(2)}) async-start(), calls=%async_computation | async-start | bytes 5242880 | tf_op jit(solution)/shard_map/all_gather | solution.py:91
  8.9 14.8 %collective-permute-start.6 = (s32[128]{0:T(128)S(1)}, s32[128]{0:T(128)S(1)}, u32[]{:S(2)}, u32[]{:S(2)}) collective-permute-start(s32[128]{0:T(128)S(1)} %slice.54), channel_id=1, source_target_pairs={{0,4},{4,8},{8,12},{12,16},{16,20},{20,24},{24,28},{28,32},{32,36}... | collective-permute-start | bytes 1544 | tf_op jit(solution)/shard_map/ppermute | solution.py:15
  11.0 12.7 %collective-permute-start.7 = (s32[128]{0:T(128)S(1)}, s32[128]{0:T(128)S(1)}, u32[]{:S(2)}, u32[]{:S(2)}) collective-permute-start(s32[128]{0:T(128)S(1)} %slice.56), channel_id=1, source_target_pairs={{4,0},{8,4},{12,8},{16,12},{20,16},{24,20},{28,24},{32,28},{36,32}... | collective-permute-start | bytes 1544 | tf_op jit(solution)/shard_map/ppermute | solution.py:15
  17.9 8.4 %collective-permute-start.1 = (s32[512]{0:T(512)}, s32[512]{0:T(512)S(1)}, u32[]{:S(2)}, u32[]{:S(2)}) collective-permute-start(s32[512]{0:T(512)} %param.12), channel_id=1, source_target_pairs={{0,4},{4,8},{8,12},{12,16},{16,20},{20,24},{24,28},{28,32},{32,36}... | collective-permute-start | bytes 6152 | tf_op jit(solution)/shard_map/ppermute | solution.py:15
  62.1 3.4 %copy-start.1 = (bf16[512,4096]{1,0:T(8,128)(2,1)S(1)}, bf16[512,4096]{1,0:T(8,128)(2,1)}, u32[]{:S(2)}) copy-start(bf16[512,4096]{1,0:T(8,128)(2,1)} %all-gather.2.cloned.1.call-done) | copy-start | bytes 12582916
  72.0 19.1 %copy-start.2 = (bf16[512,4096]{1,0:T(8,128)(2,1)S(1)}, bf16[512,4096]{1,0:T(8,128)(2,1)}, u32[]{:S(2)}) copy-start(bf16[512,4096]{1,0:T(8,128)(2,1)} %all-gather.2.cloned.1.call-done) | copy-start | bytes 12582916
  72.0 19.1 %copy-start.4 = (bf16[4096,512]{1,0:T(8,128)(2,1)S(1)}, bf16[4096,512]{1,0:T(8,128)(2,1)}, u32[]{:S(2)}) copy-start(bf16[4096,512]{1,0:T(8,128)(2,1)} %param.9) | copy-start | bytes 12582916
  76.4 26.5 %collective-permute-start = (bf16[512,256]{1,0:T(8,128)(2,1)S(1)}, bf16[512,256]{1,0:T(8,128)(2,1)S(1)}, u32[]{:S(2)}, u32[]{:S(2)}) collective-permute-start(bf16[512,256]{1,0:T(8,128)(2,1)S(1)} %convolution_convert_fusion), channel_id=1, source_target_pairs={{0,4},{4,8},{8,12},{12,16},{16,20},{20,24},{24,28},{28,32},{32,36}... | collective-permute-start | bytes 786440 | tf_op jit(solution)/shard_map/ppermute | solution.py:15
  78.3 15.6 %collective-permute-start.8 = (bf16[128,256]{1,0:T(8,128)(2,1)S(1)}, bf16[128,256]{1,0:T(8,128)(2,1)S(1)}, u32[]{:S(2)}, u32[]{:S(2)}) collective-permute-start(bf16[128,256]{1,0:T(8,128)(2,1)S(1)} %bitcast.54), channel_id=1, source_target_pairs={{0,4},{4,8},{8,12},{12,16},{16,20},{20,24},{24,28},{28,32},{32,36}... | collective-permute-start | bytes 196616 | tf_op jit(solution)/shard_map/ppermute | solution.py:15
  81.8 19.3 %collective-permute-start.9 = (bf16[128,256]{1,0:T(8,128)(2,1)S(1)}, bf16[128,256]{1,0:T(8,128)(2,1)S(1)}, u32[]{:S(2)}, u32[]{:S(2)}) collective-permute-start(bf16[128,256]{1,0:T(8,128)(2,1)S(1)} %bitcast.53), channel_id=1, source_target_pairs={{4,0},{8,4},{12,8},{16,12},{20,16},{24,20},{28,24},{32,28},{36,32}... | collective-permute-start | bytes 196616 | tf_op jit(solution)/shard_map/ppermute | solution.py:15
  87.3 15.5 %collective-permute-start.2 = (bf16[512,256]{1,0:T(8,128)(2,1)S(1)}, bf16[512,256]{1,0:T(8,128)(2,1)S(1)}, u32[]{:S(2)}, u32[]{:S(2)}) collective-permute-start(bf16[512,256]{1,0:T(8,128)(2,1)S(1)} %bitcast.44), channel_id=1, source_target_pairs={{0,4},{4,8},{8,12},{12,16},{16,20},{20,24},{24,28},{28,32},{32,36}... | collective-permute-start | bytes 786440 | tf_op jit(solution)/shard_map/ppermute | solution.py:15
  89.2 12.0 %collective-permute-start.10 = (bf16[128,256]{1,0:T(8,128)(2,1)S(1)}, bf16[128,256]{1,0:T(8,128)(2,1)S(1)}, u32[]{:S(2)}, u32[]{:S(2)}) collective-permute-start(bf16[128,256]{1,0:T(8,128)(2,1)S(1)} %get-tuple-element.47), channel_id=1, source_target_pairs={{0,4},{4,8},{8,12},{12,16},{16,20},{20,24},{24,28},{28,32},{32,36}... | collective-permute-start | bytes 196616 | tf_op jit(solution)/shard_map/ppermute | solution.py:15
  94.0 8.9 %collective-permute-start.11 = (bf16[128,256]{1,0:T(8,128)(2,1)S(1)}, bf16[128,256]{1,0:T(8,128)(2,1)S(1)}, u32[]{:S(2)}, u32[]{:S(2)}) collective-permute-start(bf16[128,256]{1,0:T(8,128)(2,1)S(1)} %get-tuple-element.48), channel_id=1, source_target_pairs={{4,0},{8,4},{12,8},{16,12},{20,16},{24,20},{28,24},{32,28},{36,32}... | collective-permute-start | bytes 196616 | tf_op jit(solution)/shard_map/ppermute | solution.py:15
  114.8 5.4 %collective-permute-start.3 = (bf16[128,512]{1,0:T(8,128)(2,1)S(1)}, bf16[128,512]{1,0:T(8,128)(2,1)S(1)}, u32[]{:S(2)}, u32[]{:S(2)}) collective-permute-start(bf16[128,512]{1,0:T(8,128)(2,1)S(1)} %copy.43), channel_id=1, source_target_pairs={{0,1},{1,0},{2,3},{3,2},{4,5},{5,4},{6,7},{7,6},{8,9},{9,8},{10,11... | collective-permute-start | bytes 393224 | tf_op jit(solution)/shard_map/ppermute | solution.py:150
  115.9 6.6 %collective-permute-start.4 = (bf16[128,512]{1,0:T(8,128)(2,1)S(1)}, bf16[128,512]{1,0:T(8,128)(2,1)S(1)}, u32[]{:S(2)}, u32[]{:S(2)}) collective-permute-start(bf16[128,512]{1,0:T(8,128)(2,1)S(1)} %copy.44), channel_id=1, source_target_pairs={{0,2},{1,3},{2,0},{3,1},{4,6},{5,7},{6,4},{7,5},{8,10},{9,11},{10,... | collective-permute-start | bytes 393224 | tf_op jit(solution)/shard_map/ppermute | solution.py:150
  117.9 6.3 %collective-permute-start.5 = (bf16[128,512]{1,0:T(8,128)(2,1)S(1)}, bf16[128,512]{1,0:T(8,128)(2,1)S(1)}, u32[]{:S(2)}, u32[]{:S(2)}) collective-permute-start(bf16[128,512]{1,0:T(8,128)(2,1)S(1)} %copy.45), channel_id=1, source_target_pairs={{0,3},{1,2},{2,1},{3,0},{4,7},{5,6},{6,5},{7,4},{8,11},{9,10},{10,... | collective-permute-start | bytes 393224 | tf_op jit(solution)/shard_map/ppermute | solution.py:150
  124.1 0.8 copy-start.3
Sparse Core Ops, SparseCore 0:
  9.8 52.2 all-gather.1
